TPU v7x, 32 devices: a whole 2x2x4 slice. The times are simulated.
32 devices in a mesh: rows: 8 (over z, y), cls: 4 (over x, core).
Axes of the slice: x: 2, y: 2, z: 4, core: 2. Of those that a mesh axis runs over, the one named last changes fastest.
Arguments:
- features: bfloat16 [6144, 2048], P('rows', 'cls'), may hold values from -32 to 32
- prototypes: bfloat16 [2048, 16384], P('rows', 'cls'), may hold values from -1 to 1
Outputs:
- grad_proto: float32 [2048, 16384], P('rows', 'cls')
All inputs are finite; a program needn't handle non-finite values.
Results may differ from a plain program's by a relative error of at most 0.02.
Values may be sent and summed in bfloat16 or wider, within the bound.
A program may use at most 128 MiB of HBM per device.

v0:
```python
import jax
import jax.numpy as jnp
from jax import lax
from jax.sharding import PartitionSpec as P

ITERS = 3
code_temp = 0.2
loss_temp = 0.3


def local(features, prototypes):
    gathered = lax.all_gather(features, "cls", axis=1, tiled=True)
    local_rows = gathered.shape[0]
    local_classes = prototypes.shape[1]
    balance_ratio = float(local_rows * lax.axis_size("rows")) / float(
        local_classes * lax.axis_size("cls")
    )
    columns = gathered
    scores = jnp.dot(
        columns,
        lax.all_gather(prototypes, "rows", axis=0, tiled=True),
        preferred_element_type=jnp.float32,
    )
    local_top = jnp.max(scores, axis=1)
    row_top = lax.pmax(local_top, "cls")
    shifted = scores - row_top[:, None]
    exp_codes = jnp.exp(shifted / code_temp)
    exp_loss = jnp.exp(shifted / loss_temp)
    sink_total, soft_total = lax.psum(
        (jnp.sum(exp_codes, axis=1), jnp.sum(exp_loss, axis=1)), "cls"
    )
    codes = exp_codes / sink_total[:, None]
    for sweep in range(ITERS):
        col_mass = lax.psum(jnp.sum(codes, axis=0), "rows")
        codes = codes * (balance_ratio / col_mass)[None, :]
        row_mass = lax.psum(jnp.sum(codes, axis=1), "cls")
        codes = codes / row_mass[:, None]
    probs_loss = exp_loss / soft_total[:, None]
    slope = ((probs_loss - codes) / loss_temp).astype(jnp.bfloat16)
    columns = gathered
    return lax.psum_scatter(
        lax.dot_general(
            columns, slope, (((0,), (0,)), ((), ())), preferred_element_type=jnp.float32
        ).astype(jnp.bfloat16),
        "rows",
        scatter_dimension=0,
        tiled=True,
    ).astype(jnp.float32)


def solution(mesh):
    return jax.shard_map(
        local,
        mesh=mesh,
        in_specs=(P("rows", "cls"), P("rows", "cls")),
        out_specs=P("rows", "cls"),
        check_vma=False,
    )
```

profile of v0, /device:TPU:0, one launch (start us, length us, event | category | flops | bytes accessed | tf_op | source)
XLA Modules:
  0.0 786.4 jit_solution(6704144554605490783)
XLA Ops:
  6.5 0.7 all-gather.3.cloned.1.call-update
  7.3 0.7 all-gather.5.cloned.1.call-update
  8.0 0.0 reduce-scatter.2.cloned.1.call-start
  8.1 32.1 %all-gather.3.cloned.1.call-done = bf16[768,2048]{1,0:T(8,128)(2,1)} async-done(((bf16[768,512]{1,0:T(8,128)(2,1)}), bf16[768,2048]{1,0:T(8,128)(2,1)}) %all-gather.3.cloned.1.call-update) | async-done | bytes 3145744 | tf_op jit(solution)/shard_map/all_gather | solution.py:12
  40.2 229.8 %all-gather.5.cloned.1.call-done = bf16[2048,4096]{1,0:T(8,128)(2,1)} async-done(((bf16[256,4096]{1,0:T(8,128)(2,1)}), bf16[2048,4096]{1,0:T(8,128)(2,1)}) %all-gather.5.cloned.1.call-update) | async-done | bytes 16777232 | tf_op jit(solution)/shard_map/all_gather | solution.py:21
  270.0 20.3 %fusion.8 = (f32[768]{0:T(1024)S(1)}, f32[768,4096]{1,0:T(8,128)}) fusion(bf16[768,2048]{1,0:T(8,128)(2,1)} %all-gather.3.cloned.1.call-done, bf16[2048,4096]{1,0:T(8,128)(2,1)} %all-gather.5.cloned.1.call-done), kind=kOutput, calls=%fused_computation.19 | convolution fusion | flops 12888046592 | bytes 32508928 | tf_op jit(solution)/shard_map/dot_general | solution.py:19
  290.3 6.1 pmax.7
  296.4 7.1 fusion
  303.5 6.1 psum.57
  309.7 11.3 %fusion.6 = (f32[4096]{0:T(1024)S(1)}, f32[768,4096]{1,0:T(8,128)}) fusion(f32[768]{0:T(1024)S(1)} %psum.57, f32[768,4096]{1,0:T(8,128)} %get-tuple-element.14, f32[768]{0:T(1024)S(1)} %pmax.7), kind=kLoop, calls=%fused_computation.18 | loop fusion | flops 12578816 | bytes 25188352 | tf_op jit(solution)/shard_map/reduce_sum | solution.py:34
  320.9 34.6 %psum.58 = f32[4096]{0:T(1024)S(1)} all-reduce(f32[4096]{0:T(1024)S(1)} %get-tuple-element.11), channel_id=1, replica_groups=mesh['rows'=8,'cls'=4] {'rows'}, use_global_device_ids=true, to_apply=%region_7.0 | all-reduce | flops 4096 | bytes 32768 | tf_op jit(solution)/shard_map/psum | solution.py:34
  355.6 5.5 multiply_reduce_fusion.2
  361.1 5.8 psum.59
  366.8 6.4 fusion.4
  373.3 33.2 %psum.60 = f32[4096]{0:T(1024)S(1)} all-reduce(f32[4096]{0:T(1024)S(1)} %fusion.4), channel_id=1, replica_groups=mesh['rows'=8,'cls'=4] {'rows'}, use_global_device_ids=true, to_apply=%region_11.0 | all-reduce | flops 4096 | bytes 32768 | tf_op jit(solution)/shard_map/psum | solution.py:34
  406.5 6.0 multiply_reduce_fusion.1
  412.4 5.8 psum.61
  418.2 11.3 %fusion.5 = (f32[4096]{0:T(1024)S(1)}, f32[768,4096]{1,0:T(8,128)}) fusion(f32[768]{0:T(1024)S(1)} %psum.61, f32[4096]{0:T(1024)S(1)} %broadcast_divide_fusion.1, f32[768]{0:T(1024)S(1)} %psum.59, f32[768,4096]{1,0:T(8,128)} %get-tuple-element.12, f32[4096]{0:T(1024)S(1)} %broadcast_divide_fusion.2), kind=kLoop, calls=%fused_computation.17 | loop fusion | flops 15724544 | bytes 25221120 | tf_op jit(solution)/shard_map/reduce_sum | solution.py:34
  429.5 33.2 %psum.62 = f32[4096]{0:T(1024)S(1)} all-reduce(f32[4096]{0:T(1024)S(1)} %get-tuple-element.9), channel_id=1, replica_groups=mesh['rows'=8,'cls'=4] {'rows'}, use_global_device_ids=true, to_apply=%region_15.0 | all-reduce | flops 4096 | bytes 32768 | tf_op jit(solution)/shard_map/psum | solution.py:34
  462.7 5.5 multiply_reduce_fusion
  468.2 5.9 all-reduce
  474.1 22.6 %convert_bitcast_fusion = bf16[2048,4096]{0,1:T(8,128)(2,1)} fusion(bf16[768,2048]{1,0:T(8,128)(2,1)S(1)} %copy-done, f32[768,4096]{1,0:T(8,128)} %get-tuple-element.10, f32[768,4096]{1,0:T(8,128)} %get-tuple-element.14, f32[768]{0:T(1024)S(1)} %get-tuple-element.7, f32[4096]{0:T(1024)S(1)} %broadcast_divide_fusion, f32[768]{0:T(1024)S(1)} %get-tuple-element.8, ...), kind=kOutput, calls=%fused_computation | convolution fusion | flops 12918456320 | bytes 45114368 | tf_op jit(solution)/shard_map/dot_general | solution.py:42
  496.8 278.8 %reduce-scatter.2.cloned.1.call-done = bf16[256,4096]{0,1:T(8,128)(2,1)} async-done(((bf16[2048,4096]{0,1:T(8,128)(2,1)}), bf16[256,4096]{0,1:T(8,128)(2,1)}) %reduce-scatter.2.cloned.1.call-update) | async-done | bytes 2097168 | tf_op jit(solution)/shard_map/reduce_scatter | solution.py:41
  775.6 4.3 copy.3
  (8 shorter events, 0.1 us)
Async XLA Ops:
  6.5 33.6 %all-gather.3.cloned.1.call-start = ((), (), s32[]{:S(2)}) async-start(), calls=%async_computation.1 | async-start | bytes 3932160 | tf_op jit(solution)/shard_map/all_gather | solution.py:12
  7.3 262.7 %all-gather.5.cloned.1.call-start = ((), (), s32[]{:S(2)}) async-start(), calls=%async_computation.2 | async-start | bytes 18874368 | tf_op jit(solution)/shard_map/all_gather | solution.py:21
  8.0 767.6 %reduce-scatter.2.cloned.1.call-start = ((), (), s32[]{:S(2)}) async-start(), calls=%async_computation.3 | async-start | bytes 18874368 | tf_op jit(solution)/shard_map/reduce_scatter | solution.py:41
  429.5 44.6 %copy-start = (bf16[768,2048]{1,0:T(8,128)(2,1)S(1)}, bf16[768,2048]{1,0:T(8,128)(2,1)}, u32[]{:S(2)}) copy-start(bf16[768,2048]{1,0:T(8,128)(2,1)} %all-gather.3.cloned.1.call-done) | copy-start | bytes 9437188
Sparse Core Ops, SparseCore 0:
  8.9 31.2 all-gather.2
  42.3 227.6 all-gather.4
  496.9 278.6 reduce-scatter.1
where the time goes:
time: 787 us; the launch traced here: 786 us
  waiting for transfers between devices  542 us (69%)
  blocking collectives  131 us (17%)
  other arithmetic  53.1 us (7%)
  matrix products  42.9 us (5%)
  between operations  13.1 us (2%)
    reduce_scatter x1, waiting for transfers between devices, local(): lax.psum_scatter(lax.dot_general(columns, slope, (((0,), (0,)), ((), ()))...  279 us
    all_gather x1, waiting for transfers between devices, local(): lax.all_gather(prototypes, 'rows', axis=0, tiled=True)  230 us
    psum x3, blocking collectives, local(): col_mass = lax.psum(jnp.sum(codes, axis=0), 'rows')  101 us
    all_gather x1, waiting for transfers between devices, local(): gathered = lax.all_gather(features, 'cls', axis=1, tiled=True)  32.1 us
    reduce_sum x3, other arithmetic, local(): col_mass = lax.psum(jnp.sum(codes, axis=0), 'rows')  29 us
    dot_general x1, matrix products, local(): lax.dot_general(columns, slope, (((0,), (0,)), ((), ())), preferred_eleme...  22.6 us
    dot_general x1, matrix products, local(): jnp.dot(columns, lax.all_gather(prototypes, 'rows', axis=0, tiled=True),...  20.3 us
    psum x3, blocking collectives, local(): row_mass = lax.psum(jnp.sum(codes, axis=1), 'cls')  17.4 us
  transfers between devices with their start and end apart: 3, of which 3 were waited for; matrix products, arithmetic and copies ran while one was open for 0% of the time, Pallas kernels for 0%

commit v1 on v0

--- a/solution.py
+++ b/solution.py
@@ -8,8 +8,21 @@
 loss_temp = 0.3
 
 
+def gather_around(x, axis, dim):
+    length, index, rows = (lax.axis_size(axis), lax.axis_index(axis), x.shape[dim])
+    upward = [(i, (i + 1) % length) for i in range(length)]
+    out = jnp.zeros((*x.shape[:dim], length * rows, *x.shape[dim + 1 :]), x.dtype)
+    current = x
+    for step in range(length):
+        holder = (index - step) % length
+        out = lax.dynamic_update_slice_in_dim(out, current, holder * rows, axis=dim)
+        if step < length - 1:
+            current = lax.ppermute(current, axis, upward)
+    return out
+
+
 def local(features, prototypes):
-    gathered = lax.all_gather(features, "cls", axis=1, tiled=True)
+    gathered = gather_around(features, "cls", 1)
     local_rows = gathered.shape[0]
     local_classes = prototypes.shape[1]
     balance_ratio = float(local_rows * lax.axis_size("rows")) / float(

time: 787 us -> 760 us (0.966)
  waiting for transfers between devices: 542 us -> 504 us
    all_gather x1, waiting for transfers between devices: 230 us -> 195 us  [local(): lax.all_gather(prototypes, 'rows', axis=0, tiled=True)]
    all_gather x1 -> x0, waiting for transfers between devices: 32.1 us -> none  [local(): gathered = lax.all_gather(features, 'cls', axis=1, tiled=True)]
    ppermute x0 -> x3, waiting for transfers between devices: none -> 30.9 us  [gather_around(): current = lax.ppermute(current, axis, upward)]
  transfers between devices with their start and end apart: 3 -> 5, of which waited for: 3 -> 5; matrix products, arithmetic and copies ran while one was open for 0% -> 1% of each run, Pallas kernels for 0% -> 0%
where the time goes in v1:
time: 760 us; the launch traced here: 759 us
  waiting for transfers between devices  504 us (66%)
  blocking collectives  130 us (17%)
  other arithmetic  57.2 us (8%)
  matrix products  46.8 us (6%)
  between operations  13.5 us (2%)
    reduce_scatter x1, waiting for transfers between devices, local(): lax.psum_scatter(lax.dot_general(columns, slope, (((0,), (0,)), ((), ()))...  278 us
    all_gather x1, waiting for transfers between devices, local(): lax.all_gather(prototypes, 'rows', axis=0, tiled=True)  195 us
    psum x3, blocking collectives, local(): col_mass = lax.psum(jnp.sum(codes, axis=0), 'rows')  101 us
    ppermute x3, waiting for transfers between devices, gather_around(): current = lax.ppermute(current, axis, upward)  30.9 us
    reduce_sum x3, other arithmetic, local(): col_mass = lax.psum(jnp.sum(codes, axis=0), 'rows')  29 us
    dot_general x1, matrix products, local(): lax.dot_general(columns, slope, (((0,), (0,)), ((), ())), preferred_eleme...  27.4 us
    dot_general x1, matrix products, local(): jnp.dot(columns, lax.all_gather(prototypes, 'rows', axis=0, tiled=True),...  19.4 us
    psum x3, blocking collectives, local(): row_mass = lax.psum(jnp.sum(codes, axis=1), 'cls')  17.4 us
  transfers between devices with their start and end apart: 5, of which 5 were waited for; matrix products, arithmetic and copies ran while one was open for 1% of the time, Pallas kernels for 0%

profile of v1, /device:TPU:0, one launch (start us, length us, event | category | flops | bytes accessed | tf_op | source)
XLA Modules:
  0.0 759.2 jit_solution(4585161158435188429)
XLA Ops:
  7.8 11.8 %collective-permute-done = bf16[768,512]{1,0:T(8,128)(2,1)S(1)} collective-permute-done((bf16[768,512]{1,0:T(8,128)(2,1)}, bf16[768,512]{1,0:T(8,128)(2,1)S(1)}, u32[]{:S(2)}, u32[]{:S(2)}) %collective-permute-start) | collective-permute-done | bytes 786464 | tf_op jit(solution)/shard_map/ppermute | solution.py:20
  20.5 11.5 %collective-permute-done.1 = bf16[768,512]{1,0:T(8,128)(2,1)} collective-permute-done((bf16[768,512]{1,0:T(8,128)(2,1)S(1)}, bf16[768,512]{1,0:T(8,128)(2,1)}, u32[]{:S(2)}, u32[]{:S(2)}) %collective-permute-start.1) | collective-permute-done | bytes 786464 | tf_op jit(solution)/shard_map/ppermute | solution.py:20
  33.7 1.3 constant_dynamic-update-slice_fusion.2
  36.2 7.6 collective-permute-done.2
  45.0 194.8 %all-gather.2.cloned.1.call-done = bf16[2048,4096]{1,0:T(8,128)(2,1)} async-done(((bf16[256,4096]{1,0:T(8,128)(2,1)}), bf16[2048,4096]{1,0:T(8,128)(2,1)}) %all-gather.2.cloned.1.call-update) | async-done | bytes 16777232 | tf_op jit(solution)/shard_map/all_gather | solution.py:34
  239.8 19.4 %fusion.8 = (f32[768]{0:T(1024)S(1)}, f32[768,4096]{1,0:T(8,128)}) fusion(bf16[768,2048]{1,0:T(8,128)(2,1)S(1)} %constant_dynamic-update-slice_fusion, bf16[2048,4096]{1,0:T(8,128)(2,1)} %all-gather.2.cloned.1.call-done), kind=kOutput, calls=%fused_computation.23 | convolution fusion | flops 12888046592 | bytes 32508928 | tf_op jit(solution)/shard_map/dot_general | solution.py:32
  259.2 6.1 pmax.7
  265.4 7.1 fusion
  272.5 6.1 psum.57
  278.6 11.3 %fusion.6 = (f32[4096]{0:T(1024)S(1)}, f32[768,4096]{1,0:T(8,128)}) fusion(f32[768]{0:T(1024)S(1)} %psum.57, f32[768,4096]{1,0:T(8,128)} %get-tuple-element.14, f32[768]{0:T(1024)S(1)} %pmax.7), kind=kLoop, calls=%fused_computation.22 | loop fusion | flops 12578816 | bytes 25188352 | tf_op jit(solution)/shard_map/reduce_sum | solution.py:47
  289.9 34.6 %psum.58 = f32[4096]{0:T(1024)S(1)} all-reduce(f32[4096]{0:T(1024)S(1)} %get-tuple-element.11), channel_id=1, replica_groups=mesh['rows'=8,'cls'=4] {'rows'}, use_global_device_ids=true, to_apply=%region_7.8 | all-reduce | flops 4096 | bytes 32768 | tf_op jit(solution)/shard_map/psum | solution.py:47
  324.6 5.5 multiply_reduce_fusion.2
  330.0 5.8 psum.59
  335.8 6.4 fusion.4
  342.3 33.2 %psum.60 = f32[4096]{0:T(1024)S(1)} all-reduce(f32[4096]{0:T(1024)S(1)} %fusion.4), channel_id=1, replica_groups=mesh['rows'=8,'cls'=4] {'rows'}, use_global_device_ids=true, to_apply=%region_11.12 | all-reduce | flops 4096 | bytes 32768 | tf_op jit(solution)/shard_map/psum | solution.py:47
  375.4 6.0 multiply_reduce_fusion.1
  381.4 5.8 psum.61
  387.2 11.3 %fusion.5 = (f32[4096]{0:T(1024)S(1)}, f32[768,4096]{1,0:T(8,128)}) fusion(f32[768]{0:T(1024)S(1)} %psum.61, f32[4096]{0:T(1024)S(1)} %broadcast_divide_fusion.1, f32[768]{0:T(1024)S(1)} %psum.59, f32[768,4096]{1,0:T(8,128)} %get-tuple-element.12, f32[4096]{0:T(1024)S(1)} %broadcast_divide_fusion.2), kind=kLoop, calls=%fused_computation.21 | loop fusion | flops 15724544 | bytes 25221120 | tf_op jit(solution)/shard_map/reduce_sum | solution.py:47
  398.5 33.0 %psum.62 = f32[4096]{0:T(1024)S(1)} all-reduce(f32[4096]{0:T(1024)S(1)} %get-tuple-element.9), channel_id=1, replica_groups=mesh['rows'=8,'cls'=4] {'rows'}, use_global_device_ids=true, to_apply=%region_15.16 | all-reduce | flops 4096 | bytes 32768 | tf_op jit(solution)/shard_map/psum | solution.py:47
  431.4 5.5 multiply_reduce_fusion
  436.9 5.9 all-reduce
  442.8 27.4 %convolution_convert_fusion = bf16[2048,4096]{1,0:T(8,128)(2,1)} fusion(bf16[768,2048]{1,0:T(8,128)(2,1)S(1)} %constant_dynamic-update-slice_fusion, f32[768,4096]{1,0:T(8,128)} %get-tuple-element.10, f32[768,4096]{1,0:T(8,128)} %get-tuple-element.14, f32[768]{0:T(1024)S(1)} %get-tuple-element.7, f32[4096]{0:T(1024)S(1)} %broadcast_divide_fusion, ...), kind=kOutput, calls=%fused_computation | convolution fusion | flops 12918456320 | bytes 45114368 | tf_op jit(solution)/shard_map/dot_general | solution.py:55
  470.2 278.0 %reduce-scatter.2.cloned.1.call-done = bf16[256,4096]{1,0:T(8,128)(2,1)} async-done(((bf16[2048,4096]{1,0:T(8,128)(2,1)}), bf16[256,4096]{1,0:T(8,128)(2,1)}) %reduce-scatter.2.cloned.1.call-update) | async-done | bytes 2097168 | tf_op jit(solution)/shard_map/reduce_scatter | solution.py:54
  748.2 4.1 convert_element_type.11
  (16 shorter events, 6.3 us)
Async XLA Ops:
  6.5 233.3 %all-gather.2.cloned.1.call-start = ((), (), s32[]{:S(2)}) async-start(), calls=%async_computation.1 | async-start | bytes 18874368 | tf_op jit(solution)/shard_map/all_gather | solution.py:34
  7.3 741.0 %reduce-scatter.2.cloned.1.call-start = ((), (), s32[]{:S(2)}) async-start(), calls=%async_computation.2 | async-start | bytes 18874368 | tf_op jit(solution)/shard_map/reduce_scatter | solution.py:54
  7.3 12.3 %collective-permute-start = (bf16[768,512]{1,0:T(8,128)(2,1)}, bf16[768,512]{1,0:T(8,128)(2,1)S(1)}, u32[]{:S(2)}, u32[]{:S(2)}) collective-permute-start(bf16[768,512]{1,0:T(8,128)(2,1)} %param.2), channel_id=1, source_target_pairs={{0,1},{1,2},{2,3},{3,0},{4,5},{5,6},{6,7},{7,4},{8,9},{9,10},{10,1... | collective-permute-start | bytes 2359304 | tf_op jit(solution)/shard_map/ppermute | solution.py:20
  19.6 0.9 copy-start
  20.5 11.5 %collective-permute-start.1 = (bf16[768,512]{1,0:T(8,128)(2,1)S(1)}, bf16[768,512]{1,0:T(8,128)(2,1)}, u32[]{:S(2)}, u32[]{:S(2)}) collective-permute-start(bf16[768,512]{1,0:T(8,128)(2,1)S(1)} %collective-permute-done), channel_id=1, source_target_pairs={{0,1},{1,2},{2,3},{3,0},{4,5},{5,6},{6,7},{7,4},{8,9},{9,10},{10,1... | collective-permute-start | bytes 2359304 | tf_op jit(solution)/shard_map/ppermute | solution.py:20
  32.0 11.7 %collective-permute-start.2 = (bf16[768,512]{1,0:T(8,128)(2,1)}, bf16[768,512]{1,0:T(8,128)(2,1)}, u32[]{:S(2)}, u32[]{:S(2)}) collective-permute-start(bf16[768,512]{1,0:T(8,128)(2,1)} %collective-permute-done.1), channel_id=1, source_target_pairs={{0,1},{1,2},{2,3},{3,0},{4,5},{5,6},{6,7},{7,4},{8,9},{9,10},{10,1... | collective-permute-start | bytes 2359304 | tf_op jit(solution)/shard_map/ppermute | solution.py:20
Sparse Core Ops, SparseCore 0:
  9.5 230.3 all-gather.1
  470.3 277.8 reduce-scatter.1
